TPU v7x, 256 devices: a whole 4x4x8 slice. The times are simulated.
256 devices in a mesh: ment: 64 (over z, x, core), ent: 4 (over y).
Axes of the slice: x: 4, y: 4, z: 8, core: 2. Of those that a mesh axis runs over, the one named last changes fastest.
Arguments:
- hidden_in: bfloat16 [4096, 32, 1024], P('ment'), may hold values from -16 to 16
- w_qkv: bfloat16 [1024, 3, 1024], P(None, None, 'ent'), may hold values from -0.1875 to 0.1875
- w_out: bfloat16 [1024, 1024], P('ent'), may hold values from -0.1875 to 0.1875
- ln_gain: float32 [1024], replicated, may hold values from 0.5 to 1.5
- ln_bias: float32 [1024], replicated, may hold values from -3 to 3
- table: bfloat16 [32, 256, 1024], P('ent'), may hold values from -0.5 to 0.5
- key_len: int32 [4096], P('ment'), may hold values from 4 to 32
- gold_block: int32 [4096], P('ment'), may hold values from 0 to 31
- gold_row: int32 [4096], P('ment'), may hold values from 0 to 255
- neg_blocks: int32 [64, 4], P('ment'), may hold values from 0 to 31, as said below
Outputs:
- grad_hidden: bfloat16 [4096, 32, 1024], P(('ment', 'ent'))
- grad_qkv: float32 [1024, 3, 1024], P('ment', None, 'ent')
- grad_wo: float32 [1024, 1024], P('ent', 'ment')
- grad_ln: float32 [2, 1024], P(None, 'ment')
- grad_table: float32 [32, 256, 1024], P('ent', 'ment')
Inputs may be any that keep to these rules, and one draw needn't show every extreme that they name: `neg_blocks`: each row lists 4 different blocks.
All inputs are finite; a program needn't handle non-finite values.
Results may differ from a plain program's by a relative error of at most 0.028.
Values may be sent and summed in bfloat16 or wider, within the bound.
A program may use at most 128 MiB of HBM per device.

v0:
```python
import jax
import jax.numpy as jnp
from jax import lax
from jax.sharding import PartitionSpec as P

HD = 64
ln_eps = 1e-06


def contract(left, right, left_dim, right_dim):
    return lax.dot_general(
        left, right, (((left_dim,), (right_dim,)), ((), ())), preferred_element_type=jnp.float32
    )


def on_device(
    hidden_in, w_qkv, w_out, ln_gain, ln_bias, table, key_len, gold_block, gold_row, neg_blocks
):
    ment_rows, seq_len, width = hidden_in.shape
    local_cols = w_qkv.shape[2]
    local_heads = local_cols // HD
    own_blocks, block_rows = (table.shape[0], table.shape[1])
    score_scale = HD ** (-0.5)
    owner = lax.axis_index("ent")
    first_block = owner * own_blocks
    cls_rows = hidden_in[:, 0, :]
    w_query = w_qkv[:, 0, :]
    w_keyval = w_qkv[:, 1:, :].reshape(width, 2 * local_cols)
    query = jnp.dot(cls_rows, w_query, preferred_element_type=jnp.float32).astype(jnp.bfloat16)
    keyval = jnp.dot(
        hidden_in.reshape(ment_rows * seq_len, width), w_keyval, preferred_element_type=jnp.float32
    )
    keyval = keyval.astype(jnp.bfloat16).reshape(ment_rows, seq_len, 2, local_heads, HD)
    key_heads = keyval[:, :, 0]
    value_heads = keyval[:, :, 1]
    query_heads = query.reshape(ment_rows, local_heads, HD)
    attention_scores = (
        jnp.einsum("ybn,yqbn->ybq", query_heads, key_heads, preferred_element_type=jnp.float32)
        * score_scale
    )
    valid = (jnp.arange(seq_len, dtype=jnp.int32)[None, :] < key_len[:, None]).astype(jnp.float32)
    expo = jnp.exp(attention_scores) * valid[:, None, :]
    probs = expo / jnp.sum(expo, axis=-1, keepdims=True)
    probability_half = probs.astype(jnp.bfloat16)
    context_rows = jnp.einsum(
        "qjp,qpjb->qjb", probability_half, value_heads, preferred_element_type=jnp.float32
    )
    context_rows = context_rows.reshape(ment_rows, local_cols).astype(jnp.bfloat16)
    attn_part = jnp.dot(context_rows, w_out, preferred_element_type=jnp.float32)
    local_block = gold_block - first_block
    owned = (local_block >= 0) & (local_block < own_blocks)
    safe_block = jnp.clip(local_block, 0, own_blocks - 1)
    flat_table = table.reshape(own_blocks * block_rows, width)
    picked = flat_table[safe_block * block_rows + gold_row]
    picked = jnp.where(owned[:, None], picked.astype(jnp.float32), 0.0)
    attn_out, gold_sum = (
        lax.psum(attn_part.astype(jnp.bfloat16), "ent").astype(jnp.float32),
        lax.psum(picked.astype(jnp.bfloat16), "ent").astype(jnp.float32),
    )
    golds = gold_sum.astype(jnp.bfloat16)
    resid = cls_rows.astype(jnp.float32) + attn_out
    centre = resid - jnp.mean(resid, axis=-1, keepdims=True)
    rstd = lax.rsqrt(jnp.mean(centre * centre, axis=-1, keepdims=True) + ln_eps)
    normed = centre * rstd
    embed = (normed * ln_gain + ln_bias).astype(jnp.bfloat16)
    inbatch = contract(embed, golds, 1, 1)
    negscore = contract(embed, flat_table, 1, 1)
    block_ids = first_block + jnp.arange(own_blocks, dtype=jnp.int32)
    listed = jnp.any(neg_blocks[0][:, None] == block_ids[None, :], axis=0).astype(jnp.float32)
    row_mask = jnp.repeat(listed, block_rows)
    neg_part = jnp.sum(jnp.exp(negscore) * row_mask[None, :], axis=1)
    neg_total = lax.psum(neg_part, "ent")
    lse = jnp.log(jnp.sum(jnp.exp(inbatch), axis=1) + neg_total)
    eye = jnp.eye(ment_rows, dtype=jnp.float32)
    w_inb = (jnp.exp(inbatch - lse[:, None]) - eye).astype(jnp.bfloat16)
    w_neg = (jnp.exp(negscore - lse[:, None]) * row_mask[None, :]).astype(jnp.bfloat16)
    embed_part = jnp.dot(w_neg, flat_table, preferred_element_type=jnp.float32)
    d_embed = jnp.dot(w_inb, golds, preferred_element_type=jnp.float32) + lax.psum(
        embed_part.astype(jnp.bfloat16), "ent"
    ).astype(jnp.float32)
    ln_terms = jnp.stack([jnp.sum(d_embed * normed, axis=0), jnp.sum(d_embed, axis=0)])
    upper = d_embed * ln_gain
    d_resid = rstd * (
        upper
        - jnp.mean(upper, axis=-1, keepdims=True)
        - normed * jnp.mean(upper * normed, axis=-1, keepdims=True)
    )
    d_resid_bf = d_resid.astype(jnp.bfloat16)
    wo_term = contract(context_rows, d_resid_bf, 0, 0)
    grad_wo, grad_ln = (
        lax.psum_scatter(wo_term, "ment", scatter_dimension=1, tiled=True),
        lax.psum_scatter(ln_terms, "ment", scatter_dimension=1, tiled=True),
    )
    d_context = contract(d_resid_bf, w_out, 1, 1).astype(jnp.bfloat16)
    context_head_gradient = d_context.reshape(ment_rows, local_heads, HD)
    probability_gradient = jnp.einsum(
        "ybn,yqbn->ybq", context_head_gradient, value_heads, preferred_element_type=jnp.float32
    )
    score_gradient = probs * (
        probability_gradient - jnp.sum(probs * probability_gradient, axis=-1, keepdims=True)
    )
    query_gradient = (
        jnp.einsum("qjp,qpjb->qjb", score_gradient, key_heads, preferred_element_type=jnp.float32)
        * score_scale
    )
    query_gradient = query_gradient.reshape(ment_rows, local_cols).astype(jnp.bfloat16)
    key_gradient = (
        jnp.einsum("ryk,ryo->rkyo", score_gradient, query_heads, preferred_element_type=jnp.float32)
        * score_scale
    )
    value_gradient = jnp.einsum(
        "ryk,ryo->rkyo", probability_half, context_head_gradient, preferred_element_type=jnp.float32
    )
    d_keyval = (
        jnp.stack([key_gradient, value_gradient], axis=2)
        .reshape(ment_rows, seq_len, 2 * local_cols)
        .astype(jnp.bfloat16)
    )
    flat_grad = d_keyval.reshape(ment_rows * seq_len, 2 * local_cols)
    count = lax.axis_size("ment") * (width // lax.axis_size("ment"))
    kv_term = contract(hidden_in.reshape(ment_rows * seq_len, count), flat_grad, 0, 0)
    query_term = contract(hidden_in[:, 0, :], query_gradient, 0, 0)
    grad_qkv = lax.psum_scatter(
        jnp.concatenate([query_term[:, None, :], kv_term.reshape(count, 2, local_cols)], axis=1),
        "ment",
        scatter_dimension=0,
        tiled=True,
    )
    share = ment_rows // lax.axis_size("ent")
    grad_part = d_keyval.reshape(share * lax.axis_size("ent") * seq_len, 2 * local_cols)
    token_term = contract(grad_part, w_keyval, 1, 1).reshape(
        share * lax.axis_size("ent"), seq_len, width
    )
    summed = lax.psum_scatter(
        token_term.at[:, 0, :].add(contract(query_gradient, w_query, 1, 1)).astype(jnp.bfloat16),
        "ent",
        scatter_dimension=0,
        tiled=True,
    ).astype(jnp.float32)
    resid_mine = lax.dynamic_slice_in_dim(d_resid, owner * share, share, 0)
    grad_hidden = summed.at[:, 0, :].add(resid_mine).astype(jnp.bfloat16)
    gold_terms = contract(w_inb, embed, 0, 0)
    weight_blocks = w_neg.reshape(ment_rows, own_blocks, block_rows)
    count = lax.axis_size("ment") * (block_rows // lax.axis_size("ment"))
    neg_term = jnp.einsum("mbr,md->rbd", weight_blocks, embed, preferred_element_type=jnp.float32)
    inside = owned & (gold_row >= 0) & (gold_row < count)
    row_slot = jnp.where(inside, gold_row, count)
    reduced = lax.psum_scatter(
        neg_term.at[row_slot, safe_block].add(gold_terms, mode="drop"),
        "ment",
        scatter_dimension=0,
        tiled=True,
    )
    grad_table = jnp.transpose(reduced, (1, 0, 2))
    return (grad_hidden, grad_qkv, grad_wo, grad_ln, grad_table)


def solution(mesh):
    placed = (
        P("ment", None, None),
        P(None, None, "ent"),
        P("ent", None),
        P(),
        P(),
        P("ent", None, None),
        P("ment"),
        P("ment"),
        P("ment"),
        P("ment", None),
    )
    return jax.shard_map(
        on_device,
        mesh=mesh,
        in_specs=placed,
        out_specs=(
            P(("ment", "ent"), None, None),
            P("ment", None, "ent"),
            P("ent", "ment"),
            P(None, "ment"),
            P("ent", "ment", None),
        ),
        check_vma=False,
    )
```

profile of v0, /device:TPU:8, one launch (start us, length us, event | category | flops | bytes accessed | tf_op | source)
XLA Modules:
  0.0 713.5 jit_solution(6832385997085273812)
XLA Ops:
  7.2 0.7 compare_and_fusion
  7.9 0.7 compare_select_fusion.2
  8.6 0.7 fusion.34
  9.4 1.4 slice.60
  10.8 2.3 fusion.60
  13.2 1.2 convolution_convert_fusion.4
  14.6 4.5 convolution_convert_fusion
  19.1 3.7 reshape.170
  22.8 4.8 slice_bitcast_fusion
  27.6 1.3 copy-done.7
  29.0 1.2 fusion.6
  30.6 6.0 fusion.13
  36.6 1.0 copy-done.3
  37.8 0.8 copy.43
  38.6 2.3 fusion.2
  41.1 3.5 gather_fusion
  44.6 0.7 select_convert_fusion
  45.4 0.9 convolution_convert_fusion.2
  46.5 48.6 %all-reduce.7.cloned.1.call-done = (bf16[64,1024]{1,0:T(8,128)(2,1)}, bf16[64,1024]{1,0:T(8,128)(2,1)}) async-done(((bf16[64,1024]{1,0:T(8,128)(2,1)}, bf16[64,1024]{1,0:T(8,128)(2,1)}), (bf16[64,1024]{1,0:T(8,128)(2,1)}, bf16[64,1024]{1,0:T(8,128)(2,1)})) %all-reduce.7.cloned.1.call-update) | async-done | bytes 262160 | tf_op jit(solution)/shard_map/psum | solution.py:58
  95.1 1.1 fusion.28
  96.1 1.1 multiply_reduce_fusion.3
  97.3 1.0 add_convert_fusion
  98.3 1.1 exponential_reduce_fusion
  99.4 3.7 multiply_reduce_fusion
  103.1 9.4 %psum.30 = f32[64]{0:T(128)S(1)} all-reduce(f32[64]{0:T(128)S(1)} %get-tuple-element.58), channel_id=1, replica_groups=mesh['ment'=64,'ent'=4] {'ent'}, use_global_device_ids=true, to_apply=%region_8.9 | all-reduce | flops 64 | bytes 512 | tf_op jit(solution)/shard_map/psum | solution.py:72
  112.7 3.7 convolution_convert_fusion.1
  116.8 3.3 copy.34
  120.1 2.5 reshape.198
  122.7 39.3 %all-reduce.5.cloned.1.call-done = bf16[64,1024]{1,0:T(8,128)(2,1)} async-done(((bf16[64,1024]{1,0:T(8,128)(2,1)}), bf16[64,1024]{1,0:T(8,128)(2,1)}) %all-reduce.5.cloned.1.call-update) | async-done | bytes 131088 | tf_op jit(solution)/shard_map/psum | solution.py:78
  162.0 1.3 multiply_reduce_fusion.1
  164.0 2.8 fusion
  166.8 1.4 copy.47
  168.2 2.4 fusion.9
  170.6 0.8 copy.48
  171.4 2.3 fusion.4
  173.9 1.3 fusion.15
  175.2 2.5 multiply_bitcast_fusion.1
  177.7 2.5 multiply_bitcast_fusion
  180.2 5.4 maximum_convert_fusion
  185.6 6.8 convert_element_type.118
  192.4 4.5 fusion.61
  196.9 3.2 copy-done.2
  200.5 6.1 scatter-add.14
  206.6 6.0 convert_element_type.121
  213.3 4.5 convolution_bitcast_fusion
  217.7 9.0 %copy.38 = f32[256,8,1024]{2,1,0:T(8,128)} copy(f32[256,8,1024]{0,2,1:T(8,128)} %convolution_bitcast_fusion) | data formatting | bytes 16777216 | tf_op jit(solution)/shard_map/mbr,md->rbd/transpose | solution.py:145
  226.9 10.5 %scatter_fusion = f32[256,8,1024]{2,1,0:T(8,128)} fusion(f32[256,8,1024]{2,1,0:T(8,128)} %copy.38, s32[64]{0:T(128)S(1)} %fusion.38, f32[64,1024]{1,0:T(8,128)S(1)} %fusion.39), kind=kCustom, calls=%fused_computation.1 | custom fusion | flops 65536 | bytes 786944 | tf_op jit(solution)/shard_map/scatter-add | solution.py:149
  237.5 0.7 copy-done.9
  238.4 1.3 copy.35
  239.8 1.3 fusion.31
  241.1 0.6 copy-done.5
  241.8 6.0 fusion.62
  247.8 1.9 copy.36
  249.7 3.2 pad_maximum_fusion
  253.0 0.6 copy-done.20
  253.6 0.6 dynamic-slice.16
  254.9 129.7 %all-reduce = f32[2,1024]{1,0:T(2,128)S(1)} all-reduce(f32[2,1024]{1,0:T(2,128)S(1)} %pad_maximum_fusion.1), channel_id=5, replica_groups=mesh['ment'=64,'ent'=4] {'ment'}, use_global_device_ids=true, to_apply=%region_18.19.clone | all-reduce | flops 2048 | bytes 16384
  384.6 0.6 constant_dynamic-slice_fusion
  385.2 1.5 convert_element_type.122
  387.3 1.1 convert_element_type.123
  388.4 31.0 %reduce-scatter.12.cloned.1.call-done = f32[4,8,1024]{2,1,0:T(8,128)} async-done(((f32[256,8,1024]{2,1,0:T(8,128)}), f32[4,8,1024]{2,1,0:T(8,128)}) %reduce-scatter.12.cloned.1.call-update) | async-done | bytes 131088 | tf_op jit(solution)/shard_map/reduce_scatter | solution.py:148
  419.4 1.6 copy.39
  421.1 140.4 %reduce-scatter.10.cloned.1.call-done = f32[256,16]{0,1:T(8,128)} async-done(((f32[256,1024]{0,1:T(8,128)}), f32[256,16]{0,1:T(8,128)}) %reduce-scatter.10.cloned.1.call-update) | async-done | bytes 16400 | tf_op jit(solution)/shard_map/reduce_scatter | solution.py:91
  561.5 145.2 %reduce-scatter.8.cloned.1.call-done = f32[16,3,256]{2,0,1:T(8,128)} async-done(((f32[1024,3,256]{2,0,1:T(8,128)}), f32[16,3,256]{2,0,1:T(8,128)}) %reduce-scatter.8.cloned.1.call-update) | async-done | bytes 49168 | tf_op jit(solution)/shard_map/reduce_scatter | solution.py:123
  (84 shorter events, 4.9 us)
Async XLA Ops:
  7.2 38.2 %copy-start = (bf16[256,1024]{1,0:T(8,128)(2,1)S(1)}, bf16[256,1024]{1,0:T(8,128)(2,1)}, u32[]{:S(2)}) copy-start(bf16[256,1024]{1,0:T(8,128)(2,1)} %param.16) | copy-start | bytes 1572868
  7.2 87.9 %all-reduce.7.cloned.1.call-start = ((), (), s32[]{:S(2)}) async-start(), calls=%async_computation.9 | async-start | bytes 524288 | tf_op jit(solution)/shard_map/psum | solution.py:58
  27.6 1.4 copy-start.7
  36.6 1.0 copy-start.3
  38.6 7.7 %copy-start.19 = (s32[1,4]{1,0:T(1,128)S(1)}, s32[1,4]{1,0:T(1,128)}, u32[]{:S(2)}) copy-start(s32[1,4]{1,0:T(1,128)} %param.23) | copy-start | bytes 52
  40.9 56.4 %copy-start.15 = (f32[1024]{0:T(1024)S(1)}, f32[1024]{0:T(1024)}, u32[]{:S(2)}) copy-start(f32[1024]{0:T(1024)} %param.17) | copy-start | bytes 12292
  40.9 56.4 %copy-start.16 = (f32[1024]{0:T(1024)S(1)}, f32[1024]{0:T(1024)}, u32[]{:S(2)}) copy-start(f32[1024]{0:T(1024)} %param.18) | copy-start | bytes 12292
  41.1 62.1 %copy-start.10 = (bf16[64,256]{1,0:T(8,128)(2,1)}, bf16[64,256]{1,0:T(8,128)(2,1)S(1)}, u32[]{:S(2)}) copy-start(bf16[64,256]{1,0:T(8,128)(2,1)S(1)} %convert_element_type.103) | copy-start | bytes 98308
  46.2 115.7 %all-reduce.5.cloned.1.call-start = ((), (), s32[]{:S(2)}) async-start(), calls=%async_computation.4 | async-start | bytes 262144 | tf_op jit(solution)/shard_map/psum | solution.py:78
  99.4 62.6 %copy-start.13 = (f32[64,64]{0,1:T(8,128)}, f32[64,64]{0,1:T(8,128)S(1)}, u32[]{:S(2)}) copy-start(f32[64,64]{0,1:T(8,128)S(1)} %get-tuple-element.57) | copy-start | bytes 49156
  116.4 268.8 %reduce-scatter.6.cloned.1.call-start = ((), (), s32[]{:S(2)}) async-start(), calls=%async_computation.5 | async-start | bytes 5242880 | tf_op jit(solution)/shard_map/reduce_scatter | solution.py:134
  116.8 45.2 %copy-start.6 = (bf16[64,1024]{1,0:T(8,128)(2,1)S(1)}, bf16[64,1024]{1,0:T(8,128)(2,1)}, u32[]{:S(2)}) copy-start(bf16[64,1024]{1,0:T(8,128)(2,1)} %get-tuple-element.49) | copy-start | bytes 393220
  116.8 45.2 %copy-start.12 = (bf16[64,1024]{1,0:T(8,128)(2,1)S(1)}, bf16[64,1024]{1,0:T(8,128)(2,1)}, u32[]{:S(2)}) copy-start(bf16[64,1024]{1,0:T(8,128)(2,1)} %get-tuple-element.48) | copy-start | bytes 393220
  173.8 6.3 copy-start.8
  192.4 4.5 copy-start.4
  196.9 3.2 copy-start.2
  212.6 0.7 copy-start.17
  212.6 0.7 copy-start.18
  212.6 206.8 %reduce-scatter.12.cloned.1.call-start = ((), (), s32[]{:S(2)}) async-start(), calls=%async_computation.8 | async-start | bytes 8519680 | tf_op jit(solution)/shard_map/reduce_scatter | solution.py:148
  217.7 9.0 %copy-start.14 = (f32[64,64]{0,1:T(8,128)S(1)}, f32[64,64]{0,1:T(8,128)}, u32[]{:S(2)}) copy-start(f32[64,64]{0,1:T(8,128)} %copy-done.13) | copy-start | bytes 49156
  237.4 0.8 copy-start.9
  237.4 2.4 copy-start.11
  237.4 324.1 %reduce-scatter.10.cloned.1.call-start = ((), (), s32[]{:S(2)}) async-start(), calls=%async_computation.7 | async-start | bytes 1064960 | tf_op jit(solution)/shard_map/reduce_scatter | solution.py:91
  239.8 2.0 copy-start.5
  241.1 465.6 %reduce-scatter.8.cloned.1.call-start = ((), (), s32[]{:S(2)}) async-start(), calls=%async_computation.6 | async-start | bytes 3194880 | tf_op jit(solution)/shard_map/reduce_scatter | solution.py:123
  252.9 0.7 copy-start.20
  385.2 321.4 %copy-start.1 = (bf16[256,1024]{1,0:T(8,128)(2,1)S(1)}, bf16[256,1024]{1,0:T(8,128)(2,1)}, u32[]{:S(2)}) copy-start(bf16[256,1024]{1,0:T(8,128)(2,1)} %param.16) | copy-start | bytes 1572868
Sparse Core Ops, SparseCore 0:
  46.4 48.6 all-reduce.6
  116.5 45.4 all-reduce.4
  212.7 49.6 reduce-scatter.5
  267.1 152.3 reduce-scatter.11
  423.8 137.6 reduce-scatter.9
  566.0 140.5 reduce-scatter.7
where the time goes:
time: 715 us; the launch traced here: 714 us
  waiting for transfers between devices  405 us (57%)
  blocking collectives  139 us (19%)
  local copies, waits for them, and re-layouts  62.6 us (9%)
  other arithmetic  48.3 us (7%)
  matrix products  43.3 us (6%)
  between operations  15.2 us (2%)
    reduce_scatter x1, waiting for transfers between devices, on_device(): lax.psum_scatter(jnp.concatenate([query_term[:, None, :], kv_term.reshape...  145 us
    reduce_scatter x1, waiting for transfers between devices, on_device(): lax.psum_scatter(wo_term, 'ment', scatter_dimension=1, tiled=True)  140 us
    unnamed x1, blocking collectives  130 us
    psum x1, waiting for transfers between devices, on_device(): lax.psum(picked.astype(jnp.bfloat16), 'ent').astype(jnp.float32)  48.6 us
    psum x1, waiting for transfers between devices, on_device(): lax.psum(embed_part.astype(jnp.bfloat16), 'ent').astype(jnp.float32)  39.3 us
    reduce_scatter x1, waiting for transfers between devices, on_device(): lax.psum_scatter(neg_term.at[row_slot, safe_block].add(gold_terms, mode='...  31 us
    dot_general x9, matrix products, contract(): lax.dot_general(left, right, (((left_dim,), (right_dim,)), ((), ())), pre...  18.7 us
  transfers between devices with their start and end apart: 6, of which 5 were waited for; matrix products, arithmetic and copies ran while one was open for 7% of the time, Pallas kernels for 0%

commit v1 on v0

--- a/solution.py
+++ b/solution.py
@@ -75,8 +75,8 @@
     w_inb = (jnp.exp(inbatch - lse[:, None]) - eye).astype(jnp.bfloat16)
     w_neg = (jnp.exp(negscore - lse[:, None]) * row_mask[None, :]).astype(jnp.bfloat16)
     embed_part = jnp.dot(w_neg, flat_table, preferred_element_type=jnp.float32)
-    d_embed = jnp.dot(w_inb, golds, preferred_element_type=jnp.float32) + lax.psum(
-        embed_part.astype(jnp.bfloat16), "ent"
+    d_embed = jnp.dot(w_inb, golds, preferred_element_type=jnp.float32) + jnp.sum(
+        lax.all_gather(embed_part.astype(jnp.bfloat16), "ent"), axis=0
     ).astype(jnp.float32)
     ln_terms = jnp.stack([jnp.sum(d_embed * normed, axis=0), jnp.sum(d_embed, axis=0)])
     upper = d_embed * ln_gain

time: 715 us -> 682 us (0.954)
  waiting for transfers between devices: 405 us -> 364 us
  blocking collectives: 139 us -> 148 us
    psum x1 -> x0, waiting for transfers between devices: 39.3 us -> none  [on_device(): lax.psum(embed_part.astype(jnp.bfloat16), 'ent').astype(jnp.float32)]
    all_gather x0 -> x1, blocking collectives: none -> 12.2 us  [on_device(): lax.all_gather(embed_part.astype(jnp.bfloat16), 'ent')]
  transfers between devices with their start and end apart: 6 -> 5, of which waited for: 5 -> 4; matrix products, arithmetic and copies ran while one was open for 7% -> 7% of each run, Pallas kernels for 0% -> 0%
where the time goes in v1:
time: 682 us; the launch traced here: 680 us
  waiting for transfers between devices  364 us (53%)
  blocking collectives  148 us (22%)
  local copies, waits for them, and re-layouts  62.3 us (9%)
  other arithmetic  49.1 us (7%)
  matrix products  41.7 us (6%)
  between operations  14.9 us (2%)
    reduce_scatter x1, waiting for transfers between devices, on_device(): lax.psum_scatter(jnp.concatenate([query_term[:, None, :], kv_term.reshape...  146 us
    reduce_scatter x1, waiting for transfers between devices, on_device(): lax.psum_scatter(wo_term, 'ment', scatter_dimension=1, tiled=True)  141 us
    unnamed x1, blocking collectives  127 us
    psum x1, waiting for transfers between devices, on_device(): lax.psum(picked.astype(jnp.bfloat16), 'ent').astype(jnp.float32)  42.6 us
    reduce_scatter x1, waiting for transfers between devices, on_device(): lax.psum_scatter(neg_term.at[row_slot, safe_block].add(gold_terms, mode='...  34.2 us
    dot_general x9, matrix products, contract(): lax.dot_general(left, right, (((left_dim,), (right_dim,)), ((), ())), pre...  18.6 us
  transfers between devices with their start and end apart: 5, of which 4 were waited for; matrix products, arithmetic and copies ran while one was open for 7% of the time, Pallas kernels for 0%

profile of v1, /device:TPU:8, one launch (start us, length us, event | category | flops | bytes accessed | tf_op | source)
XLA Modules:
  0.0 680.2 jit_solution(8918334153003437755)
XLA Ops:
  7.2 0.7 compare_and_fusion
  7.9 0.7 compare_select_fusion.2
  8.6 0.7 fusion.34
  9.4 1.4 slice.60
  10.8 2.3 fusion.60
  13.2 1.2 convolution_convert_fusion.4
  14.6 4.5 convolution_convert_fusion
  19.1 3.7 reshape.170
  22.8 4.8 slice_bitcast_fusion
  27.6 1.3 copy-done.7
  29.0 1.2 fusion.6
  30.6 6.0 fusion.13
  36.6 1.0 copy-done.3
  37.8 0.8 copy.43
  38.6 2.3 fusion.2
  41.1 3.5 gather_fusion
  44.6 0.7 select_convert_fusion
  45.4 0.9 convolution_convert_fusion.2
  46.6 3.3 copy.34
  49.9 2.5 reshape.199
  52.5 42.6 %all-reduce.4.cloned.1.call-done = (bf16[64,1024]{1,0:T(8,128)(2,1)}, bf16[64,1024]{1,0:T(8,128)(2,1)}) async-done(((bf16[64,1024]{1,0:T(8,128)(2,1)}, bf16[64,1024]{1,0:T(8,128)(2,1)}), (bf16[64,1024]{1,0:T(8,128)(2,1)}, bf16[64,1024]{1,0:T(8,128)(2,1)})) %all-reduce.4.cloned.1.call-update) | async-done | bytes 262160 | tf_op jit(solution)/shard_map/psum | solution.py:58
  95.1 1.1 fusion.28
  96.1 1.1 multiply_reduce_fusion.3
  97.3 1.0 add_convert_fusion
  98.3 1.1 exponential_reduce_fusion
  99.4 3.7 multiply_reduce_fusion
  103.1 9.4 %psum.23 = f32[64]{0:T(128)S(1)} all-reduce(f32[64]{0:T(128)S(1)} %get-tuple-element.58), channel_id=1, replica_groups=mesh['ment'=64,'ent'=4] {'ent'}, use_global_device_ids=true, to_apply=%region_8.9 | all-reduce | flops 64 | bytes 512 | tf_op jit(solution)/shard_map/psum | solution.py:72
  112.7 3.1 convolution_convert_fusion.1
  115.8 12.2 %all-gather = bf16[256,1024]{1,0:T(8,128)(2,1)S(1)} all-gather(bf16[64,1024]{1,0:T(8,128)(2,1)S(1)} %convolution_convert_fusion.1), channel_id=2, replica_groups=mesh['ment'=64,'ent'=4] {'ent'}, dimensions={0}, use_global_device_ids=true | all-gather | bytes 655360 | tf_op jit(solution)/shard_map/all_gather | solution.py:79
  128.6 0.8 subtract_multiply_fusion
  129.9 2.8 fusion
  132.7 1.4 copy.47
  134.1 2.4 fusion.9
  136.5 0.8 copy.48
  137.3 2.3 fusion.4
  139.8 1.3 fusion.15
  141.1 2.5 multiply_bitcast_fusion.1
  143.6 2.5 multiply_bitcast_fusion
  146.1 5.4 maximum_convert_fusion
  151.5 6.6 convert_element_type.120
  158.1 4.5 fusion.61
  162.6 3.2 copy-done.2
  166.2 6.1 scatter-add.14
  172.3 6.0 convert_element_type.123
  178.9 4.5 convolution_bitcast_fusion
  183.4 9.0 %copy.38 = f32[256,8,1024]{2,1,0:T(8,128)} copy(f32[256,8,1024]{0,2,1:T(8,128)} %convolution_bitcast_fusion) | data formatting | bytes 16777216 | tf_op jit(solution)/shard_map/mbr,md->rbd/transpose | solution.py:145
  192.6 10.5 %scatter_fusion = f32[256,8,1024]{2,1,0:T(8,128)} fusion(f32[256,8,1024]{2,1,0:T(8,128)} %copy.38, s32[64]{0:T(128)S(1)} %fusion.38, f32[64,1024]{1,0:T(8,128)S(1)} %fusion.39), kind=kCustom, calls=%fused_computation.1 | custom fusion | flops 65536 | bytes 786944 | tf_op jit(solution)/shard_map/scatter-add | solution.py:149
  203.2 0.7 copy-done.9
  204.2 1.3 copy.35
  205.5 1.3 fusion.31
  206.9 0.6 copy-done.5
  207.5 5.9 fusion.62
  213.4 1.9 copy.36
  215.3 3.2 pad_maximum_fusion
  218.6 0.6 copy-done.23
  219.2 0.6 dynamic-slice.16
  220.5 126.7 %all-reduce = f32[2,1024]{1,0:T(2,128)S(1)} all-reduce(f32[2,1024]{1,0:T(2,128)S(1)} %pad_maximum_fusion.1), channel_id=6, replica_groups=mesh['ment'=64,'ent'=4] {'ment'}, use_global_device_ids=true, to_apply=%region_18.19.clone | all-reduce | flops 2048 | bytes 16384
  347.2 0.6 constant_dynamic-slice_fusion
  347.8 1.5 convert_element_type.124
  349.9 1.1 convert_element_type.125
  351.0 34.2 %reduce-scatter.12.cloned.1.call-done = f32[4,8,1024]{2,1,0:T(8,128)} async-done(((f32[256,8,1024]{2,1,0:T(8,128)}), f32[4,8,1024]{2,1,0:T(8,128)}) %reduce-scatter.12.cloned.1.call-update) | async-done | bytes 131088 | tf_op jit(solution)/shard_map/reduce_scatter | solution.py:148
  385.2 1.6 copy.39
  386.9 141.0 %reduce-scatter.10.cloned.1.call-done = f32[256,16]{0,1:T(8,128)} async-done(((f32[256,1024]{0,1:T(8,128)}), f32[256,16]{0,1:T(8,128)}) %reduce-scatter.10.cloned.1.call-update) | async-done | bytes 16400 | tf_op jit(solution)/shard_map/reduce_scatter | solution.py:91
  527.9 145.8 %reduce-scatter.8.cloned.1.call-done = f32[16,3,256]{2,0,1:T(8,128)} async-done(((f32[1024,3,256]{2,0,1:T(8,128)}), f32[16,3,256]{2,0,1:T(8,128)}) %reduce-scatter.8.cloned.1.call-update) | async-done | bytes 49168 | tf_op jit(solution)/shard_map/reduce_scatter | solution.py:123
  (89 shorter events, 5.0 us)
Async XLA Ops:
  7.2 38.2 %copy-start = (bf16[256,1024]{1,0:T(8,128)(2,1)S(1)}, bf16[256,1024]{1,0:T(8,128)(2,1)}, u32[]{:S(2)}) copy-start(bf16[256,1024]{1,0:T(8,128)(2,1)} %param.16) | copy-start | bytes 1572868
  7.2 87.9 %all-reduce.4.cloned.1.call-start = ((), (), s32[]{:S(2)}) async-start(), calls=%async_computation.8 | async-start | bytes 524288 | tf_op jit(solution)/shard_map/psum | solution.py:58
  27.6 1.4 copy-start.7
  36.6 1.0 copy-start.3
  38.6 7.7 %copy-start.22 = (s32[1,4]{1,0:T(1,128)S(1)}, s32[1,4]{1,0:T(1,128)}, u32[]{:S(2)}) copy-start(s32[1,4]{1,0:T(1,128)} %param.23) | copy-start | bytes 52
  41.1 8.9 %copy-start.10 = (bf16[64,256]{1,0:T(8,128)(2,1)}, bf16[64,256]{1,0:T(8,128)(2,1)S(1)}, u32[]{:S(2)}) copy-start(bf16[64,256]{1,0:T(8,128)(2,1)S(1)} %convert_element_type.105) | copy-start | bytes 98308
  46.2 301.6 %reduce-scatter.6.cloned.1.call-start = ((), (), s32[]{:S(2)}) async-start(), calls=%async_computation.4 | async-start | bytes 5242880 | tf_op jit(solution)/shard_map/reduce_scatter | solution.py:134
  46.6 50.7 %copy-start.15 = (f32[1024]{0:T(1024)S(1)}, f32[1024]{0:T(1024)}, u32[]{:S(2)}) copy-start(f32[1024]{0:T(1024)} %param.17) | copy-start | bytes 12292
  46.6 50.7 %copy-start.16 = (f32[1024]{0:T(1024)S(1)}, f32[1024]{0:T(1024)}, u32[]{:S(2)}) copy-start(f32[1024]{0:T(1024)} %param.18) | copy-start | bytes 12292
  97.3 30.9 %copy-start.17 = (f32[64]{0:T(128)}, f32[64]{0:T(128)S(1)}, u32[]{:S(2)}) copy-start(f32[64]{0:T(128)S(1)} %add_rsqrt_fusion) | copy-start | bytes 772
  99.4 28.7 %copy-start.13 = (f32[64,64]{0,1:T(8,128)}, f32[64,64]{0,1:T(8,128)S(1)}, u32[]{:S(2)}) copy-start(f32[64,64]{0,1:T(8,128)S(1)} %get-tuple-element.57) | copy-start | bytes 49156
  112.5 15.6 %copy-start.20 = (f32[64]{0:T(128)}, f32[64]{0:T(128)S(1)}, u32[]{:S(2)}) copy-start(f32[64]{0:T(128)S(1)} %add_log_fusion) | copy-start | bytes 772
  112.7 15.5 %copy-start.6 = (bf16[64,1024]{1,0:T(8,128)(2,1)S(1)}, bf16[64,1024]{1,0:T(8,128)(2,1)}, u32[]{:S(2)}) copy-start(bf16[64,1024]{1,0:T(8,128)(2,1)} %get-tuple-element.49) | copy-start | bytes 393220
  112.7 15.5 %copy-start.12 = (bf16[64,1024]{1,0:T(8,128)(2,1)S(1)}, bf16[64,1024]{1,0:T(8,128)(2,1)}, u32[]{:S(2)}) copy-start(bf16[64,1024]{1,0:T(8,128)(2,1)} %get-tuple-element.48) | copy-start | bytes 393220
  139.8 6.3 copy-start.8
  158.1 4.5 copy-start.4
  162.6 3.2 copy-start.2
  178.3 0.7 copy-start.18
  178.3 0.7 copy-start.19
  178.3 206.9 %reduce-scatter.12.cloned.1.call-start = ((), (), s32[]{:S(2)}) async-start(), calls=%async_computation.7 | async-start | bytes 8519680 | tf_op jit(solution)/shard_map/reduce_scatter | solution.py:148
  183.4 9.0 %copy-start.14 = (f32[64,64]{0,1:T(8,128)S(1)}, f32[64,64]{0,1:T(8,128)}, u32[]{:S(2)}) copy-start(f32[64,64]{0,1:T(8,128)} %copy-done.13) | copy-start | bytes 49156
  183.4 9.0 %copy-start.21 = (f32[64]{0:T(128)S(1)}, f32[64]{0:T(128)}, u32[]{:S(2)}) copy-start(f32[64]{0:T(128)} %copy-done.20) | copy-start | bytes 772
  203.1 0.8 copy-start.9
  203.1 2.4 copy-start.11
  203.1 324.8 %reduce-scatter.10.cloned.1.call-start = ((), (), s32[]{:S(2)}) async-start(), calls=%async_computation.6 | async-start | bytes 1064960 | tf_op jit(solution)/shard_map/reduce_scatter | solution.py:91
  205.5 2.0 copy-start.5
  206.8 466.8 %reduce-scatter.8.cloned.1.call-start = ((), (), s32[]{:S(2)}) async-start(), calls=%async_computation.5 | async-start | bytes 3194880 | tf_op jit(solution)/shard_map/reduce_scatter | solution.py:123
  218.6 0.7 copy-start.23
  347.8 325.8 %copy-start.1 = (bf16[256,1024]{1,0:T(8,128)(2,1)S(1)}, bf16[256,1024]{1,0:T(8,128)(2,1)}, u32[]{:S(2)}) copy-start(bf16[256,1024]{1,0:T(8,128)(2,1)} %param.16) | copy-start | bytes 1572868
Sparse Core Ops, SparseCore 0:
  46.4 48.6 all-reduce.3
  178.4 50.2 reduce-scatter.5
  232.9 152.2 reduce-scatter.11
  390.2 137.6 reduce-scatter.9
  533.0 140.6 reduce-scatter.7
